TPU v7x, 32 devices: a whole 2x2x4 slice. The times are simulated.
32 devices in a mesh: dp: 8 (over y, x, core), mp: 4 (over z).
Axes of the slice: x: 2, y: 2, z: 4, core: 2. Of those that a mesh axis runs over, the one named last changes fastest.
Arguments:
- patches: bfloat16 [8192, 1024], P(('dp', 'mp')), as said below
- scene_ids: int32 [8192], P(('dp', 'mp')), may hold values from 0 to 7, as said below
- owner_ids: int32 [8192], P(('dp', 'mp')), may hold values from 0 to 7, as said below
- fill_slot: int32 [32768], P(('dp', 'mp')), may hold values from -1 to 511, as said below
- norm1_gain: float32 [1024], replicated, may hold values from 0.1 to 1.9
- norm1_bias: float32 [1024], replicated, may hold values from -1.75 to 1.75
- qkv_weight: bfloat16 [1024, 3, 1024], P(None, None, 'mp'), may hold values from -0.25 to 0.25
- qv_bias: float32 [2, 1024], P(None, 'mp'), may hold values from -3 to 3
- out_weight: bfloat16 [1024, 1024], P('mp'), may hold values from -1.5 to 1.5
- out_bias: float32 [1024], replicated, may hold values from -1.75 to 1.75
- norm2_gain: float32 [1024], replicated, may hold values from 0.1 to 1.9
- norm2_bias: float32 [1024], replicated, may hold values from -1.75 to 1.75
- up_weight: bfloat16 [1024, 4096], P(None, 'mp'), may hold values from -0.1875 to 0.1875
- up_bias: bfloat16 [4096], P('mp'), may hold values from -3 to 3
- down_weight: bfloat16 [4096, 1024], P('mp'), may hold values from -0.125 to 0.125
- down_bias: float32 [1024], replicated, may hold values from -1.75 to 1.75
- dec_weight: bfloat16 [1024, 512], replicated, may hold values from -0.1875 to 0.1875
- dec_bias: float32 [512], replicated, may hold values from -1.75 to 1.75
- mask_token: float32 [512], replicated, may hold values from -6 to 6
- positions: bfloat16 [32768, 512], P(('dp', 'mp')), may hold values from -6 to 6
- cotangent: bfloat16 [32768, 512], P(('dp', 'mp')), may hold values from -6 to 6
Outputs:
- decoder_in: bfloat16 [32768, 512], P(('dp', 'mp'))
- grad_patches: float32 [8192, 1024], P(('dp', 'mp'))
- grad_norm1_gain: float32 [1024], replicated
- grad_norm1_bias: float32 [1024], replicated
- grad_qkv_weight: float32 [1024, 3, 1024], P(None, None, 'mp')
- grad_qv_bias: float32 [2, 1024], P(None, 'mp')
- grad_out_weight: float32 [1024, 1024], P('mp')
- grad_out_bias: float32 [1024], replicated
- grad_norm2_gain: float32 [1024], replicated
- grad_norm2_bias: float32 [1024], replicated
- grad_up_weight: float32 [1024, 4096], P(None, 'mp')
- grad_up_bias: float32 [4096], P('mp')
- grad_down_weight: float32 [4096, 1024], P('mp')
- grad_down_bias: float32 [1024], replicated
- grad_dec_weight: float32 [1024, 512], replicated
- grad_dec_bias: float32 [512], replicated
- grad_mask_token: float32 [512], replicated
Inputs may be any that keep to these rules, and one draw needn't show every extreme that they name: `scene_ids`: within each group of 1024 rows (one dp index) scene ids start at 0 and rise by one at each scene boundary, never falling; scene 0 holds 256 to 512 rows, every other scene at least one. `owner_ids`: among the 256 rows of one device no owner is named more than 64 times; in each mp column one owner is named exactly 64 times by the rows of every device. `fill_slot`: in grid block e, slot s * 64 + r is named by exactly one cell when device (s, e % 4) has an r-th row (in row order) with owner e // 4, and by no cell otherwise. `patches`: magnitudes stay below 200.
All inputs are finite; a program needn't handle non-finite values.
Results may differ from a plain program's by a relative error of at most 0.013.
The roundings to bfloat16 on the way count: a program that leaves them out, or rounds other values in their place, can miss the bound.
Values may be sent and summed in bfloat16 or wider, within the bound.
A program may use at most 128 MiB of HBM per device.

v0:
```python
import jax
import jax.numpy as jnp
from jax import lax
from jax.sharding import PartitionSpec as P

HEAD_DIM = 64
QBLOCK = 512
NEG_FILL = -1000000000.0


def layer_norm(hidden, gain, bias_vec):
    centered = hidden - jnp.mean(hidden, axis=-1, keepdims=True)
    spread = jnp.mean(centered * centered, axis=-1, keepdims=True)
    return centered * lax.rsqrt(spread + 1e-06) * gain + bias_vec


def gelu_exact(values):
    return jax.nn.gelu(values, approximate=False)


def gather_rows(weight, data_par, model_par):
    rows, width = weight.shape
    part = rows // data_par
    mine = lax.dynamic_slice_in_dim(weight, lax.axis_index("dp") * part, part, 0)
    column = lax.all_gather(mine, "mp", axis=0)
    whole = lax.all_gather(column, "dp", axis=0)
    return whole.transpose(1, 0, 2, 3).reshape(model_par * rows, width)


def low(values):
    return values.astype(jnp.bfloat16)


def per_device(
    patches,
    scene_ids,
    owner_ids,
    fill_slot,
    norm1_gain,
    norm1_bias,
    qkv_weight,
    qv_bias,
    out_weight,
    out_bias,
    norm2_gain,
    norm2_bias,
    up_weight,
    up_bias,
    down_weight,
    down_bias,
    dec_weight,
    dec_bias,
    mask_token,
    positions,
    cotangent,
):
    row_count = patches.shape[0]
    model_par = lax.axis_size("mp")
    data_par = lax.axis_size("dp")
    group_rows = row_count * model_par
    total_rows = float(row_count * model_par * data_par)
    local_width = qkv_weight.shape[2]
    local_heads = local_width // HEAD_DIM
    score_scale = HEAD_DIM ** (-0.5)
    block_rows = min(QBLOCK, group_rows)
    block_starts = jnp.arange(group_rows // block_rows, dtype=jnp.int32) * block_rows
    capacity = 2 * row_count // data_par
    slot_count = capacity * data_par
    dec_width = dec_weight.shape[1]
    out_full = gather_rows(out_weight, data_par, model_par)
    inputs_f = patches.astype(jnp.float32)
    band_sums = lax.psum(
        (jnp.sum(inputs_f, axis=0), jnp.sum(inputs_f * inputs_f, axis=0)), ("dp", "mp")
    )
    band_mean = band_sums[0] / total_rows
    band_var = band_sums[1] / total_rows - band_mean * band_mean
    band_scale = lax.rsqrt(band_var + 1e-05)
    band_hat = (inputs_f - band_mean) * band_scale
    normed1 = layer_norm(band_hat, norm1_gain, norm1_bias).astype(jnp.bfloat16)
    norm1_all, scene_all = (
        lax.all_gather(normed1, "mp", axis=0, tiled=True),
        lax.all_gather(scene_ids, "mp", axis=0, tiled=True),
    )
    bias_three = jnp.stack([qv_bias[0], jnp.zeros_like(qv_bias[0]), qv_bias[1]])
    triples = (
        jnp.einsum("td,dcj->tcj", norm1_all, qkv_weight, preferred_element_type=jnp.float32)
        + bias_three
    ).astype(jnp.bfloat16)
    query_all = triples[:, 0].reshape(group_rows, local_heads, HEAD_DIM)
    key_all = triples[:, 1].reshape(group_rows, local_heads, HEAD_DIM)
    value_all = triples[:, 2].reshape(group_rows, local_heads, HEAD_DIM)

    def block_scores(first_row):
        query_blk = lax.dynamic_slice_in_dim(query_all, first_row, block_rows, 0)
        scene_blk = lax.dynamic_slice_in_dim(scene_all, first_row, block_rows, 0)
        scores = (
            jnp.einsum("qhd,khd->hqk", query_blk, key_all, preferred_element_type=jnp.float32)
            * score_scale
        )
        same_scene = (scene_blk[:, None] == scene_all[None, :])[None]
        return (jnp.where(same_scene, scores, NEG_FILL), query_blk)

    def attend_block(first_row):
        scores, query_blk = block_scores(first_row)
        row_max = jnp.max(scores, axis=-1, keepdims=True)
        exp_scores = jnp.exp(scores - row_max)
        row_total = jnp.sum(exp_scores, axis=-1, keepdims=True)
        softmax_w = (exp_scores / row_total).astype(jnp.bfloat16)
        mixed_rows = jnp.einsum(
            "hqk,khd->qhd", softmax_w, value_all, preferred_element_type=jnp.float32
        )
        return (mixed_rows.astype(jnp.bfloat16), (row_max + jnp.log(row_total))[..., 0])

    head_blocks, lse_blocks = lax.map(attend_block, block_starts)
    heads_out = head_blocks.reshape(group_rows, local_width)
    heads_rows = lax.all_to_all(heads_out, "mp", split_axis=0, concat_axis=1, tiled=True)
    attn_local = jnp.dot(heads_rows, out_full, preferred_element_type=jnp.float32)
    after_attn = band_hat + attn_local + out_bias
    normed2 = layer_norm(after_attn, norm2_gain, norm2_bias).astype(jnp.bfloat16)
    norm2_all = lax.all_gather(normed2, "mp", axis=0, tiled=True)
    pre_act = jnp.dot(norm2_all, up_weight, preferred_element_type=jnp.float32) + up_bias.astype(
        jnp.float32
    )
    act_rows = gelu_exact(pre_act).astype(jnp.bfloat16)
    mlp_part = low(jnp.dot(act_rows, down_weight, preferred_element_type=jnp.float32))
    proj_part = jnp.dot(mlp_part, dec_weight, preferred_element_type=jnp.float32)
    proj_sum = lax.psum_scatter(low(proj_part), "mp", scatter_dimension=0, tiled=True)
    direct = after_attn + down_bias
    projected = low(
        jnp.dot(low(direct), dec_weight, preferred_element_type=jnp.float32)
        + proj_sum.astype(jnp.float32)
        + dec_bias
    )
    owner_onehot = (owner_ids[:, None] == jnp.arange(data_par, dtype=jnp.int32)[None, :]).astype(
        jnp.int32
    )
    earlier = jnp.sum((jnp.cumsum(owner_onehot, axis=0) - owner_onehot) * owner_onehot, axis=1)
    send_slot = owner_ids * capacity + earlier
    slot_range = jnp.arange(slot_count, dtype=jnp.int32)
    send_onehot = (send_slot[:, None] == slot_range[None, :]).astype(jnp.bfloat16)
    outgoing = jnp.einsum(
        "rs,rc->sc", send_onehot, projected, preferred_element_type=jnp.float32
    ).astype(jnp.bfloat16)
    fill_onehot = (fill_slot[:, None] == slot_range[None, :]).astype(jnp.bfloat16)
    returning = jnp.einsum(
        "gs,gc->sc", fill_onehot, cotangent, preferred_element_type=jnp.float32
    ).astype(jnp.bfloat16)
    arrived, grad_back = (
        lax.all_to_all(
            outgoing.reshape(data_par, capacity, dec_width),
            "dp",
            split_axis=0,
            concat_axis=0,
            tiled=True,
        ),
        lax.all_to_all(
            returning.reshape(data_par, capacity, dec_width),
            "dp",
            split_axis=0,
            concat_axis=0,
            tiled=True,
        ),
    )
    placed = jnp.dot(
        fill_onehot, arrived.reshape(slot_count, dec_width), preferred_element_type=jnp.float32
    )
    masked = (fill_slot < 0)[:, None]
    decoder_in = (jnp.where(masked, mask_token, placed) + positions.astype(jnp.float32)).astype(
        jnp.bfloat16
    )
    grad_mask_local = jnp.sum(jnp.where(masked, cotangent.astype(jnp.float32), 0.0), axis=0)
    grad_proj = jnp.einsum(
        "rs,sc->rc",
        send_onehot,
        grad_back.reshape(slot_count, dec_width),
        preferred_element_type=jnp.float32,
    )
    grad_proj_low = grad_proj.astype(jnp.bfloat16)
    proj_grad_all = lax.all_gather(grad_proj_low, "mp", axis=0, tiled=True)
    grad_dec_local = jnp.einsum(
        "rd,rc->dc", low(direct), grad_proj_low, preferred_element_type=jnp.float32
    ) + jnp.einsum("rd,rc->dc", mlp_part, proj_grad_all, preferred_element_type=jnp.float32)
    grad_dec_bias_local = jnp.sum(grad_proj, axis=0)
    grad_block = jnp.einsum(
        "rc,dc->rd", grad_proj_low, dec_weight, preferred_element_type=jnp.float32
    )
    grad_down_bias_local = jnp.sum(low(grad_block).astype(jnp.float32), axis=0)
    grad_mlp_all = low(
        jnp.einsum("rc,dc->rd", proj_grad_all, dec_weight, preferred_element_type=jnp.float32)
    )
    grad_act = jnp.einsum(
        "tc,fc->tf", grad_mlp_all, down_weight, preferred_element_type=jnp.float32
    )
    grad_down_local = jnp.einsum(
        "tf,tc->fc", act_rows, grad_mlp_all, preferred_element_type=jnp.float32
    )
    down_sum = lax.psum(low(grad_down_local), "dp").astype(jnp.float32)
    gelu_val, gelu_back = jax.vjp(gelu_exact, pre_act)
    grad_pre = gelu_back(grad_act)[0].astype(jnp.bfloat16)
    grad_up_local = jnp.einsum("td,tf->df", norm2_all, grad_pre, preferred_element_type=jnp.float32)
    grad_up_bias_local = jnp.sum(grad_pre.astype(jnp.float32), axis=0)
    grad_norm2 = lax.psum_scatter(
        low(jnp.einsum("tf,df->td", grad_pre, up_weight, preferred_element_type=jnp.float32)),
        "mp",
        scatter_dimension=0,
        tiled=True,
    ).astype(jnp.float32)
    up_sum = lax.psum(low(grad_up_local), "dp").astype(jnp.float32)
    norm2_val, norm2_back = jax.vjp(layer_norm, after_attn, norm2_gain, norm2_bias)
    from_norm2, grad_gain2_local, grad_bias2_local = norm2_back(grad_norm2)
    grad_after = grad_block + from_norm2
    grad_attn = grad_after.astype(jnp.bfloat16)
    grad_out_bias_local = jnp.sum(grad_attn.astype(jnp.float32), axis=0)
    grad_out_rows = low(
        jnp.einsum("tj,tc->jc", heads_rows, grad_attn, preferred_element_type=jnp.float32)
    ).reshape(model_par, local_width, -1)
    out_part = lax.psum_scatter(grad_out_rows, "dp", scatter_dimension=1, tiled=True)
    out_part = lax.psum_scatter(out_part, "mp", scatter_dimension=0, tiled=True)
    out_sum = lax.all_gather(out_part[0], "dp", axis=0, tiled=True).astype(jnp.float32)
    grad_heads = lax.all_to_all(
        low(jnp.einsum("tc,jc->tj", grad_attn, out_full, preferred_element_type=jnp.float32)),
        "mp",
        split_axis=1,
        concat_axis=0,
        tiled=True,
    )
    grad_heads3 = grad_heads.reshape(group_rows, local_heads, HEAD_DIM)

    def back_block(carried, inputs):
        key_acc, value_acc = carried
        first_row, log_total = inputs
        scores, query_blk = block_scores(first_row)
        softmax_w = jnp.exp(scores - log_total[..., None])
        upstream = lax.dynamic_slice_in_dim(grad_heads3, first_row, block_rows, 0)
        value_acc = value_acc + jnp.einsum(
            "hqk,qhd->khd",
            softmax_w.astype(jnp.bfloat16),
            upstream,
            preferred_element_type=jnp.float32,
        )
        grad_probs = jnp.einsum(
            "qhd,khd->hqk", upstream, value_all, preferred_element_type=jnp.float32
        )
        inner_sum = jnp.sum(softmax_w * grad_probs, axis=-1, keepdims=True)
        grad_scores = (softmax_w * (grad_probs - inner_sum)).astype(jnp.bfloat16)
        grad_query = (
            jnp.einsum("hqk,khd->qhd", grad_scores, key_all, preferred_element_type=jnp.float32)
            * score_scale
        )
        key_acc = (
            key_acc
            + jnp.einsum("hqk,qhd->khd", grad_scores, query_blk, preferred_element_type=jnp.float32)
            * score_scale
        )
        return ((key_acc, value_acc), grad_query.astype(jnp.bfloat16))

    zero_heads = jnp.zeros((group_rows, local_heads, HEAD_DIM), jnp.float32)
    (key_grad, value_grad), query_blocks = lax.scan(
        back_block, (zero_heads, zero_heads), (block_starts, lse_blocks)
    )
    grad_triples = jnp.stack(
        [
            query_blocks.reshape(group_rows, local_width),
            key_grad.reshape(group_rows, local_width).astype(jnp.bfloat16),
            value_grad.reshape(group_rows, local_width).astype(jnp.bfloat16),
        ],
        axis=1,
    )
    grad_qkv_local = jnp.einsum(
        "td,tcj->dcj", norm1_all, grad_triples, preferred_element_type=jnp.float32
    )
    triple_sums = jnp.sum(grad_triples.astype(jnp.float32), axis=0)
    grad_qv_local = jnp.stack([triple_sums[0], triple_sums[2]])
    grad_norm1 = lax.psum_scatter(
        low(
            jnp.einsum("tcj,dcj->td", grad_triples, qkv_weight, preferred_element_type=jnp.float32)
        ),
        "mp",
        scatter_dimension=0,
        tiled=True,
    ).astype(jnp.float32)
    qkv_sum = lax.psum(low(grad_qkv_local), "dp").astype(jnp.float32)
    norm1_val, norm1_back = jax.vjp(layer_norm, band_hat, norm1_gain, norm1_bias)
    from_norm1, grad_gain1_local, grad_bias1_local = norm1_back(grad_norm1)
    grad_hat = grad_after + from_norm1
    dec_sum = lax.psum(low(grad_dec_local), ("dp", "mp")).astype(jnp.float32)
    summed_small = lax.psum((grad_qv_local, grad_up_bias_local), "dp")
    shared = lax.psum(
        (
            jnp.sum(grad_hat, axis=0),
            jnp.sum(grad_hat * band_hat, axis=0),
            grad_gain1_local,
            grad_bias1_local,
            grad_gain2_local,
            grad_bias2_local,
            grad_out_bias_local,
            grad_down_bias_local,
            grad_dec_bias_local,
            grad_mask_local,
        ),
        ("dp", "mp"),
    )
    grad_patches = band_scale * (
        grad_hat - shared[0] / total_rows - band_hat * (shared[1] / total_rows)
    )
    return (
        decoder_in,
        grad_patches,
        shared[2],
        shared[3],
        qkv_sum,
        summed_small[0],
        out_sum,
        shared[6],
        shared[4],
        shared[5],
        up_sum,
        summed_small[1],
        down_sum,
        shared[7],
        dec_sum,
        shared[8],
        shared[9],
    )


def solution(mesh):
    in_specs = (
        P(("dp", "mp"), None),
        P(("dp", "mp")),
        P(("dp", "mp")),
        P(("dp", "mp")),
        P(),
        P(),
        P(None, None, "mp"),
        P(None, "mp"),
        P("mp", None),
        P(),
        P(),
        P(),
        P(None, "mp"),
        P("mp"),
        P("mp", None),
        P(),
        P(),
        P(),
        P(),
        P(("dp", "mp"), None),
        P(("dp", "mp"), None),
    )
    out_specs = (
        P(("dp", "mp"), None),
        P(("dp", "mp"), None),
        P(),
        P(),
        P(None, None, "mp"),
        P(None, "mp"),
        P("mp", None),
        P(),
        P(),
        P(),
        P(None, "mp"),
        P("mp"),
        P("mp", None),
        P(),
        P(),
        P(),
        P(),
    )
    return jax.shard_map(
        per_device, mesh=mesh, in_specs=in_specs, out_specs=out_specs, check_vma=False
    )
```

profile of v0, /device:TPU:0, one launch (start us, length us, event | category | flops | bytes accessed | tf_op | source)
XLA Modules:
  0.0 733.2 jit_solution(15494136100213632518)
XLA Ops:
  8.6 42.1 %all-reduce.1 = (f32[1024]{0:T(1024)S(1)}, f32[1024]{0:T(1024)S(1)}) all-reduce(f32[1024]{0:T(1024)S(1)} %get-tuple-element.181, f32[1024]{0:T(1024)S(1)} %get-tuple-element.180), channel_id=1, replica_groups=mesh['dp'=8,'mp'=4] {'dp','mp'}, use_global_device_ids=true, to_apply=%region_6.7 | all-reduce | flops 2048 | bytes 16384 | tf_op jit(solution)/shard_map/psum | solution.py:72
  55.6 3.0 fusion.56
  58.6 4.1 all-to-all-start.2
  63.7 17.0 %all-gather = bf16[128,1024]{1,0:T(8,128)(2,1)} all-gather(bf16[32,1024]{1,0:T(8,128)(2,1)S(1)} %constant_dynamic-slice_fusion), channel_id=2, replica_groups=mesh['dp'=8,'mp'=4] {'mp'}, dimensions={0}, use_global_device_ids=true | all-gather | bytes 327680 | tf_op jit(solution)/shard_map/all_gather | solution.py:25
  80.8 10.5 %all-gather.3 = s32[4,1,256]{2,1,0:T(1,128)S(1)} all-gather(s32[1,1,256]{2,1,0:T(1,128)S(1)} %bitcast.166), channel_id=1, replica_groups=mesh['dp'=8,'mp'=4] {'mp'}, dimensions={0}, use_global_device_ids=true | all-gather | bytes 5120 | tf_op jit(solution)/shard_map/all_gather | solution.py:82
  92.4 13.1 %all-gather.9.cloned.1.call-done = bf16[1024,1024]{1,0:T(8,128)(2,1)} async-done(((bf16[256,1024]{1,0:T(8,128)(2,1)}), bf16[1024,1024]{1,0:T(8,128)(2,1)}) %all-gather.9.cloned.1.call-update) | async-done | bytes 2097168 | tf_op jit(solution)/shard_map/all_gather | solution.py:81
  105.5 3.9 add_convert_fusion.1
  111.2 22.3 %while.27 = (s32[]{:T(128)}, bf16[2,512,4,64]{1,3,2,0:T(8,128)(2,1)}, f32[2,4,512]{2,1,0:T(4,128)S(1)}, s32[2]{0:T(128)S(1)}, s32[1024]{0:T(1024)S(1)}, /*index=...) while((s32[]{:T(128)}, ...), condition=%wide.region_12.13_spmd, body=%wide.region_9.12_spmd.sunk | while | flops 562690048 | bytes 35203332 | solution.py:114
  118.5 3.0 fusion.170
  129.7 3.0 fusion.170
  136.7 2.9 all_to_all.32
  141.5 4.1 all-to-all-start
  145.9 2.7 fusion.102
  148.7 3.2 copy.77
  151.9 8.4 %all-to-all-done = bf16[4,256,256]{1,2,0:T(8,128)(2,1)} async-done(((bf16[4,256,256]{1,2,0:T(8,128)(2,1)}), bf16[4,256,256]{1,2,0:T(8,128)(2,1)}, u32[]{:S(2)}, u32[]{:S(2)}) %all-to-all-start) | async-done | bytes 524320 | tf_op jit(solution)/shard_map/all_to_all | solution.py:116
  165.1 13.0 %all-gather.13.cloned.1.call-done = bf16[1024,512]{1,0:T(8,128)(2,1)} async-done(((bf16[256,512]{1,0:T(8,128)(2,1)}), bf16[1024,512]{1,0:T(8,128)(2,1)}) %all-gather.13.cloned.1.call-update) | async-done | bytes 1048592 | tf_op jit(solution)/shard_map/all_gather | solution.py:179
  178.1 4.1 convolution_convert_fusion.4
  182.2 42.9 %all-gather.11.cloned.1.call-done = bf16[1024,1024]{1,0:T(8,128)(2,1)} async-done(((bf16[256,1024]{1,0:T(8,128)(2,1)}), bf16[1024,1024]{1,0:T(8,128)(2,1)}) %all-gather.11.cloned.1.call-update) | async-done | bytes 2097168 | tf_op jit(solution)/shard_map/all_gather | solution.py:120
  225.1 4.7 fusion.106
  229.9 13.9 %convert_reduce_fusion = (f32[1024]{0:T(1024)}, bf16[1024,1024]{1,0:T(8,128)(2,1)S(1)}, f32[1024,1024]{1,0:T(8,128)}) fusion(f32[1024,1024]{1,0:T(8,128)S(1)} %fusion.106, f32[1024]{0:T(1024)S(1)} %convert_element_type.184, bf16[1024,1024]{1,0:T(8,128)(2,1)S(1)} %copy-done.61, bf16[1024,1024]{1,0:T(8,128)(2,1)S(1)} %copy-done), kind=kOutput, calls=%fused_computation.48 | convolution fusion | flops 2226125824 | bytes 14688256 | tf_op jit(solution)/shard_map/tc,fc->tf/dot_general | solution.py:191
  245.2 3.7 convolution_convert_fusion.3
  248.9 42.5 %reduce-scatter.8.cloned.1.call-done = bf16[256,1024]{1,0:T(8,128)(2,1)} async-done(((bf16[1024,1024]{1,0:T(8,128)(2,1)}), bf16[256,1024]{1,0:T(8,128)(2,1)}) %reduce-scatter.8.cloned.1.call-update) | async-done | bytes 524304 | tf_op jit(solution)/shard_map/reduce_scatter | solution.py:202
  298.8 3.1 convolution_convert_fusion.2
  302.1 4.6 multiply_convert_fusion.1
  312.7 4.4 fusion.107
  317.2 3.8 convolution_convert_fusion
  322.5 3.5 all-to-all-start.3
  326.0 3.1 add_convert_fusion.2
  329.2 6.1 convolution_convert_fusion.1
  335.3 5.1 all-to-all-done.3
  343.7 30.6 %while.28 = (s32[]{:T(128)}, f32[1024,4,64]{0,2,1:T(8,128)S(1)}, f32[1024,4,64]{0,2,1:T(8,128)}, bf16[2,512,4,64]{1,3,2,0:T(8,128)(2,1)}, s32[2]{0:T(128)S(1)}, ...) while((s32[]{:T(128)}, f32[1024,4,64]{0,2,1:T(8,128)S(1)}, ...), condition=%wide.region_21.22_spmd.clone, body=%wide.region_19.21_spmd.clone.sunk | while | flops 1375729664 | bytes 84740432 | solution.py:258
  351.0 3.3 multiply_reduce_fusion.3
  366.2 3.3 multiply_reduce_fusion.3
  378.6 4.6 fusion.50
  383.9 4.6 bitcast_convert_fusion
  388.6 2.8 convolution_convert_fusion.8
  391.4 3.7 all-to-all-start.1
  396.6 110.9 %all-reduce.7.cloned.1.call-done = bf16[1024,512]{1,0:T(8,128)(2,1)} async-done(((bf16[1024,512]{1,0:T(8,128)(2,1)}), bf16[1024,512]{1,0:T(8,128)(2,1)}) %all-reduce.7.cloned.1.call-update) | async-done | bytes 1048592 | tf_op jit(solution)/shard_map/psum | solution.py:286
  507.5 2.8 convert_element_type.221
  510.4 3.1 add_convert_fusion.3
  513.7 13.4 %all-reduce.2 = (f32[2,256]{1,0:T(2,128)}, f32[1024]{0:T(1024)}) all-reduce(f32[2,256]{1,0:T(2,128)S(1)} %pad_maximum_fusion.2, f32[1024]{0:T(1024)S(1)} %copy-done.49), channel_id=1, replica_groups=mesh['dp'=8,'mp'=4] {'dp'}, use_global_device_ids=true, to_apply=%region_35.36 | all-reduce | flops 1536 | bytes 12288 | tf_op jit(solution)/shard_map/psum | solution.py:287
  527.1 82.7 %all-reduce.9.cloned.1.call-done = (bf16[1024,3,256]{2,0,1:T(8,128)(2,1)}, bf16[1024,1024]{1,0:T(8,128)(2,1)}, bf16[1024,1024]{1,0:T(8,128)(2,1)}) async-done(((bf16[1024,3,256]{2,0,1:T(8,128)(2,1)}, bf16[1024,1024]{1,0:T(8,128)(2,1)}, bf16[1024,1024]{1,0:T(8,128)(2,1)}), (bf16[1024,3,256]{2,0,1:T(8,128)(2,1)}, bf16[1024,1024]{1,0:T(8,128)(2,1)}, bf16[1024,1024]{1,0:T(8,128)(2,1)})) %all-reduce.9.cloned.1.call-update) | async-done | bytes 5767184 | tf_op jit(solution)/shard_map/psum | solution.py:282
  609.9 3.5 convert_element_type.208
  618.4 13.7 %reduce-scatter.14.cloned.1.call-done = bf16[1,32,1024]{2,1,0:T(8,128)(2,1)} async-done(((bf16[4,32,1024]{2,1,0:T(8,128)(2,1)}), bf16[1,32,1024]{2,1,0:T(8,128)(2,1)}) %reduce-scatter.14.cloned.1.call-update) | async-done | bytes 65552 | tf_op jit(solution)/shard_map/reduce_scatter | solution.py:218
  632.1 10.1 %all-gather.2 = bf16[1,256,1024]{2,1,0:T(8,128)(2,1)S(1)} all-gather(bf16[1,32,1024]{2,1,0:T(8,128)(2,1)} %reduce-scatter.14.cloned.1.call-done), channel_id=4, replica_groups=mesh['dp'=8,'mp'=4] {'dp'}, dimensions={1}, use_global_device_ids=true | all-gather | bytes 589824 | tf_op jit(solution)/shard_map/all_gather | solution.py:219
  643.2 33.0 %reduce-scatter.10.cloned.1.call-done = bf16[256,1024]{1,0:T(8,128)(2,1)} async-done(((bf16[1024,1024]{1,0:T(8,128)(2,1)}), bf16[256,1024]{1,0:T(8,128)(2,1)}) %reduce-scatter.10.cloned.1.call-update) | async-done | bytes 524304 | tf_op jit(solution)/shard_map/reduce_scatter | solution.py:274
  679.7 3.6 fusion.97
  683.4 40.7 %all-reduce = (f32[1024]{0:T(1024)S(1)}, f32[1024]{0:T(1024)S(1)}, f32[1024]{0:T(1024)}, f32[1024]{0:T(1024)}, f32[1024]{0:T(1024)}, /*index=5*/f32[1024]{0:T(10...) all-reduce(f32[1024]{0:T(1024)S(1)} %get-tuple-element.176, ...), channel_id=1, replica_groups=mesh['dp'=8,'mp'=4] {'dp','mp'}, use_global_device_ids=true, to_apply=%region_28.29 | all-reduce | flops 9216 | bytes 73728 | tf_op jit(solution)/shard_map/psum | solution.py:288
  (263 shorter events, 90.6 us)
Async XLA Ops:
  7.2 222.6 %copy-start = (bf16[1024,1024]{1,0:T(8,128)(2,1)S(1)}, bf16[1024,1024]{1,0:T(8,128)(2,1)}, u32[]{:S(2)}) copy-start(bf16[1024,1024]{1,0:T(8,128)(2,1)} %param.39) | copy-start | bytes 6291460
  7.2 73.6 %copy-start.52 = (f32[2,256]{1,0:T(2,128)S(1)}, f32[2,256]{1,0:T(2,128)}, u32[]{:S(2)}) copy-start(f32[2,256]{1,0:T(2,128)} %param.32) | copy-start | bytes 6148
  7.2 73.6 %copy-start.53 = (s32[256]{0:T(256)S(1)}, s32[256]{0:T(256)}, u32[]{:S(2)}) copy-start(s32[256]{0:T(256)} %param.26) | copy-start | bytes 3076
  7.2 84.1 %copy-start.43 = (s32[256]{0:T(256)S(1)}, s32[256]{0:T(256)}, u32[]{:S(2)}) copy-start(s32[256]{0:T(256)} %param.27) | copy-start | bytes 3076
  7.2 98.2 %all-gather.9.cloned.1.call-start = ((), (), s32[]{:S(2)}) async-start(), calls=%async_computation.9 | async-start | bytes 2621440 | tf_op jit(solution)/shard_map/all_gather | solution.py:81
  50.7 109.6 %copy-start.27 = (f32[1024]{0:T(1024)}, f32[1024]{0:T(1024)S(1)}, u32[]{:S(2)}) copy-start(f32[1024]{0:T(1024)S(1)} %get-tuple-element.257) | copy-start | bytes 12292
  50.7 109.6 %copy-start.29 = (f32[1024]{0:T(1024)}, f32[1024]{0:T(1024)S(1)}, u32[]{:S(2)}) copy-start(f32[1024]{0:T(1024)S(1)} %get-tuple-element.258) | copy-start | bytes 12292
  52.0 10.8 %copy-start.33 = (f32[256]{0:T(256)}, f32[256]{0:T(256)S(1)}, u32[]{:S(2)}) copy-start(f32[256]{0:T(256)S(1)} %broadcast_multiply_fusion.4) | copy-start | bytes 3076
  53.4 9.4 %copy-start.41 = (f32[256]{0:T(256)}, f32[256]{0:T(256)S(1)}, u32[]{:S(2)}) copy-start(f32[256]{0:T(256)S(1)} %fusion.76) | copy-start | bytes 3076
  58.6 82.9 %all-to-all-start.2 = ((bf16[8,64,512]{2,1,0:T(8,128)(2,1)}), bf16[8,64,512]{2,1,0:T(8,128)(2,1)}, u32[]{:S(2)}, u32[]{:S(2)}) async-start(bf16[8,64,512]{2,1,0:T(8,128)(2,1)} %bitcast.21), calls=%async_computation.3 | async-start | bytes 1048576 | tf_op jit(solution)/shard_map/all_to_all | solution.py:156
  62.8 85.9 %all-gather.15.cloned.1.call-start = ((), (), s32[]{:S(2)}) async-start(), calls=%async_computation.18 | async-start | bytes 2359296 | tf_op jit(solution)/shard_map/all_gather | solution.py:26
  136.7 23.6 %copy-start.2 = (bf16[256,1024]{1,0:T(8,128)(2,1)S(1)}, bf16[256,1024]{1,0:T(8,128)(2,1)}, u32[]{:S(2)}) copy-start(bf16[256,1024]{1,0:T(8,128)(2,1)} %param.25) | copy-start | bytes 1572868
  136.7 23.6 %copy-start.35 = (f32[1024]{0:T(1024)S(1)}, f32[1024]{0:T(1024)}, u32[]{:S(2)}) copy-start(f32[1024]{0:T(1024)} %param.34) | copy-start | bytes 12292
  141.5 18.8 %all-to-all-start = ((bf16[4,256,256]{1,2,0:T(8,128)(2,1)}), bf16[4,256,256]{1,2,0:T(8,128)(2,1)}, u32[]{:S(2)}, u32[]{:S(2)}) async-start(bf16[4,256,256]{1,2,0:T(8,128)(2,1)} %copy.76), calls=%async_computation | async-start | bytes 1048576 | tf_op jit(solution)/shard_map/all_to_all | solution.py:116
  145.7 32.4 %all-gather.13.cloned.1.call-start = ((), (), s32[]{:S(2)}) async-start(), calls=%async_computation.12 | async-start | bytes 1310720 | tf_op jit(solution)/shard_map/all_gather | solution.py:179
  148.6 76.5 %all-gather.11.cloned.1.call-start = ((), (), s32[]{:S(2)}) async-start(), calls=%async_computation.10 | async-start | bytes 2621440 | tf_op jit(solution)/shard_map/all_gather | solution.py:120
  148.7 15.2 %copy-start.32 = (f32[1024]{0:T(1024)S(1)}, f32[1024]{0:T(1024)}, u32[]{:S(2)}) copy-start(f32[1024]{0:T(1024)} %param.35) | copy-start | bytes 12292
  148.7 15.2 %copy-start.46 = (f32[1024]{0:T(1024)S(1)}, f32[1024]{0:T(1024)}, u32[]{:S(2)}) copy-start(f32[1024]{0:T(1024)} %param.36) | copy-start | bytes 12292
  151.9 13.1 %copy-start.50 = (bf16[1024]{0:T(1024)(128)(2,1)S(1)}, bf16[1024]{0:T(1024)(128)(2,1)}, u32[]{:S(2)}) copy-start(bf16[1024]{0:T(1024)(128)(2,1)} %param.38) | copy-start | bytes 6148
  165.0 126.5 %reduce-scatter.8.cloned.1.call-start = ((), (), s32[]{:S(2)}) async-start(), calls=%async_computation.13 | async-start | bytes 2621440 | tf_op jit(solution)/shard_map/reduce_scatter | solution.py:202
  229.8 14.0 %copy-start.13 = (f32[1024,1024]{1,0:T(8,128)}, f32[1024,1024]{1,0:T(8,128)S(1)}, u32[]{:S(2)}) copy-start(f32[1024,1024]{1,0:T(8,128)S(1)} %fusion.106) | copy-start | bytes 12582916
  229.9 15.3 %copy-start.56 = (bf16[1024,1024]{1,0:T(8,128)(2,1)S(1)}, bf16[1024,1024]{1,0:T(8,128)(2,1)}, u32[]{:S(2)}) copy-start(bf16[1024,1024]{1,0:T(8,128)(2,1)} %param.37) | copy-start | bytes 6291460
  248.8 47.9 %copy-start.14 = (bf16[256,512]{1,0:T(8,128)(2,1)S(1)}, bf16[256,512]{1,0:T(8,128)(2,1)}, u32[]{:S(2)}) copy-start(bf16[256,512]{1,0:T(8,128)(2,1)} %get-tuple-element.254) | copy-start | bytes 786436
  248.9 134.4 %reduce-scatter.12.cloned.1.call-start = ((), (), s32[]{:S(2)}) async-start(), calls=%async_computation.15 | async-start | bytes 2359296 | tf_op jit(solution)/shard_map/reduce_scatter | solution.py:217
  301.9 86.7 %reduce-scatter.6.cloned.1.call-start = ((), (), s32[]{:S(2)}) async-start(), calls=%async_computation.11 | async-start | bytes 1310720 | tf_op jit(solution)/shard_map/reduce_scatter | solution.py:127
  322.5 17.9 %all-to-all-start.3 = ((bf16[256,4,256]{2,0,1:T(8,128)(2,1)}), bf16[256,4,256]{2,0,1:T(8,128)(2,1)S(1)}, u32[]{:S(2)}, u32[]{:S(2)}) async-start(bf16[256,4,256]{2,0,1:T(8,128)(2,1)} %bitcast.160), calls=%async_computation.5 | async-start | bytes 1048576 | tf_op jit(solution)/shard_map/all_to_all | solution.py:220
  326.0 181.6 %all-reduce.7.cloned.1.call-start = ((), (), s32[]{:S(2)}) async-start(), calls=%async_computation.17 | async-start | bytes 2097152 | tf_op jit(solution)/shard_map/psum | solution.py:286
  329.1 14.5 %copy-start.5 = (bf16[1024,4,64]{0,2,1:T(8,128)(2,1)S(1)}, bf16[1024,4,64]{0,2,1:T(8,128)(2,1)}, u32[]{:S(2)}) copy-start(bf16[1024,4,64]{0,2,1:T(8,128)(2,1)} %copy-done.4) | copy-start | bytes 1572868
  329.1 14.5 %copy-start.10 = (bf16[1024,4,64]{0,2,1:T(8,128)(2,1)S(1)}, bf16[1024,4,64]{0,2,1:T(8,128)(2,1)}, u32[]{:S(2)}) copy-start(bf16[1024,4,64]{0,2,1:T(8,128)(2,1)} %get-tuple-element.484) | copy-start | bytes 1572868
  329.2 280.7 %all-reduce.9.cloned.1.call-start = ((), (), s32[]{:S(2)}) async-start(), calls=%async_computation.19 | async-start | bytes 11534336 | tf_op jit(solution)/shard_map/psum | solution.py:282
  383.2 248.9 %reduce-scatter.14.cloned.1.call-start = ((), (), s32[]{:S(2)}) async-start(), calls=%async_computation.16 | async-start | bytes 327680 | tf_op jit(solution)/shard_map/reduce_scatter | solution.py:218
  383.8 292.4 %reduce-scatter.10.cloned.1.call-start = ((), (), s32[]{:S(2)}) async-start(), calls=%async_computation.14 | async-start | bytes 2621440 | tf_op jit(solution)/shard_map/reduce_scatter | solution.py:274
  388.5 121.8 %copy-start.59 = (f32[512]{0:T(512)S(1)}, f32[512]{0:T(512)}, u32[]{:S(2)}) copy-start(f32[512]{0:T(512)} %param.43) | copy-start | bytes 6148
  391.4 119.0 %all-to-all-start.1 = ((bf16[8,64,512]{2,1,0:T(8,128)(2,1)}), bf16[8,64,512]{2,1,0:T(8,128)(2,1)S(1)}, u32[]{:S(2)}, u32[]{:S(2)}) async-start(bf16[8,64,512]{2,1,0:T(8,128)(2,1)} %bitcast.19), calls=%async_computation.2 | async-start | bytes 1048576 | tf_op jit(solution)/shard_map/all_to_all | solution.py:149
  396.6 117.2 %copy-start.49 = (f32[1024]{0:T(1024)S(1)}, f32[1024]{0:T(1024)}, u32[]{:S(2)}) copy-start(f32[1024]{0:T(1024)} %get-tuple-element.237) | copy-start | bytes 12292
  615.8 60.4 %copy-start.3 = (bf16[256,1024]{1,0:T(8,128)(2,1)S(1)}, bf16[256,1024]{1,0:T(8,128)(2,1)}, u32[]{:S(2)}) copy-start(bf16[256,1024]{1,0:T(8,128)(2,1)} %param.25) | copy-start | bytes 1572868
  615.8 60.4 %copy-start.28 = (f32[1024]{0:T(1024)S(1)}, f32[1024]{0:T(1024)}, u32[]{:S(2)}) copy-start(f32[1024]{0:T(1024)} %copy-done.27) | copy-start | bytes 12292
  615.8 60.4 %copy-start.30 = (f32[1024]{0:T(1024)S(1)}, f32[1024]{0:T(1024)}, u32[]{:S(2)}) copy-start(f32[1024]{0:T(1024)} %copy-done.29) | copy-start | bytes 12292
  615.8 60.4 %copy-start.31 = (f32[1024]{0:T(1024)S(1)}, f32[1024]{0:T(1024)}, u32[]{:S(2)}) copy-start(f32[1024]{0:T(1024)} %param.29) | copy-start | bytes 12292
  615.8 60.4 %copy-start.34 = (f32[256]{0:T(256)S(1)}, f32[256]{0:T(256)}, u32[]{:S(2)}) copy-start(f32[256]{0:T(256)} %copy-done.33) | copy-start | bytes 3076
  615.9 62.1 %copy-start.42 = (f32[256]{0:T(256)S(1)}, f32[256]{0:T(256)}, u32[]{:S(2)}) copy-start(f32[256]{0:T(256)} %copy-done.41) | copy-start | bytes 3076
  615.9 62.1 %copy-start.40 = (f32[256]{0:T(256)S(1)}, f32[256]{0:T(256)}, u32[]{:S(2)}) copy-start(f32[256]{0:T(256)} %copy-done.39) | copy-start | bytes 3076
  615.9 63.8 %copy-start.45 = (f32[256]{0:T(256)S(1)}, f32[256]{0:T(256)}, u32[]{:S(2)}) copy-start(f32[256]{0:T(256)} %copy-done.44) | copy-start | bytes 3076
  618.4 65.0 %copy-start.36 = (f32[1024]{0:T(1024)S(1)}, f32[1024]{0:T(1024)}, u32[]{:S(2)}) copy-start(f32[1024]{0:T(1024)} %get-tuple-element.171) | copy-start | bytes 12292
  618.4 65.0 %copy-start.37 = (f32[1024]{0:T(1024)S(1)}, f32[1024]{0:T(1024)}, u32[]{:S(2)}) copy-start(f32[1024]{0:T(1024)} %get-tuple-element.177) | copy-start | bytes 12292
  618.4 65.0 %copy-start.38 = (f32[1024]{0:T(1024)S(1)}, f32[1024]{0:T(1024)}, u32[]{:S(2)}) copy-start(f32[1024]{0:T(1024)} %get-tuple-element.240) | copy-start | bytes 12292
  618.4 65.0 %copy-start.51 = (f32[512]{0:T(512)S(1)}, f32[512]{0:T(512)}, u32[]{:S(2)}) copy-start(f32[512]{0:T(512)} %get-tuple-element.253) | copy-start | bytes 6148
  676.3 50.2 %copy-start.1 = (bf16[1024,1024]{1,0:T(8,128)(2,1)S(1)}, bf16[1024,1024]{1,0:T(8,128)(2,1)}, u32[]{:S(2)}) copy-start(bf16[1024,1024]{1,0:T(8,128)(2,1)} %param.39) | copy-start | bytes 6291460
  (38 other events, 116.2 us)
Sparse Core Ops, SparseCore 0:
  55.7 49.7 all-gather.8
  107.4 26.6 all-gather.14
  148.7 29.2 all-gather.12
  180.1 45.0 all-gather.10
  249.0 42.4 reduce-scatter.7
  302.0 40.2 reduce-scatter.11
  345.2 27.3 reduce-scatter.5
  378.3 129.2 all-reduce.6
  512.3 97.5 all-reduce.8
  612.0 20.0 reduce-scatter.13
  634.4 41.8 reduce-scatter.9
where the time goes:
time: 743 us; the launch traced here: 733 us
  waiting for transfers between devices  366 us (49%)
  blocking collectives  134 us (18%)
  matrix products  111 us (15%)
  other arithmetic  52.9 us (7%)
  local copies, waits for them, and re-layouts  30 us (4%)
  starting transfers between devices  16.3 us (2%)
  between operations  14.9 us (2%)
  loops' own time  8.35 us (1%)
    psum x1, waiting for transfers between devices, per_device(): dec_sum = lax.psum(low(grad_dec_local), ('dp', 'mp')).astype(jnp.float32)  111 us
    psum x1, waiting for transfers between devices, per_device(): qkv_sum = lax.psum(low(grad_qkv_local), 'dp').astype(jnp.float32)  82.7 us
    all_gather x1, waiting for transfers between devices, per_device(): norm2_all = lax.all_gather(normed2, 'mp', axis=0, tiled=True)  42.9 us
    reduce_scatter x1, waiting for transfers between devices, per_device(): lax.psum_scatter(low(jnp.einsum('tf,df->td', grad_pre, up_weight, preferr...  42.5 us
    psum x1, blocking collectives, per_device(): lax.psum((jnp.sum(inputs_f, axis=0), jnp.sum(inputs_f * inputs_f, axis=0)...  42.1 us
    psum x1, blocking collectives, per_device(): lax.psum((jnp.sum(grad_hat, axis=0), jnp.sum(grad_hat * band_hat, axis=0)...  40.7 us
    reduce_scatter x1, waiting for transfers between devices, per_device(): lax.psum_scatter(low(jnp.einsum('tcj,dcj->td', grad_triples, qkv_weight,...  33 us
    all_gather x1, blocking collectives, gather_rows(): column = lax.all_gather(mine, 'mp', axis=0)  17 us
  transfers between devices with their start and end apart: 15, of which 10 were waited for; matrix products, arithmetic and copies ran while one was open for 19% of the time, Pallas kernels for 0%

commit v1 on v0

--- a/solution.py
+++ b/solution.py
@@ -283,7 +283,7 @@
     norm1_val, norm1_back = jax.vjp(layer_norm, band_hat, norm1_gain, norm1_bias)
     from_norm1, grad_gain1_local, grad_bias1_local = norm1_back(grad_norm1)
     grad_hat = grad_after + from_norm1
-    dec_sum = lax.psum(low(grad_dec_local), ("dp", "mp")).astype(jnp.float32)
+    dec_sum = jnp.sum(lax.all_gather(low(grad_dec_local), ("dp", "mp")), axis=0).astype(jnp.float32)
     summed_small = lax.psum((grad_qv_local, grad_up_bias_local), "dp")
     shared = lax.psum(
         (

time: 743 us -> 790 us (1.063)
  waiting for transfers between devices: 366 us -> 386 us
  other arithmetic: 52.9 us -> 64.2 us
  matrix products: 111 us -> 119 us
    all_gather x0 -> x1, waiting for transfers between devices: none -> 147 us  [per_device(): lax.all_gather(low(grad_dec_local), ('dp', 'mp'))]
    psum x1 -> x0, waiting for transfers between devices: 111 us -> none  [per_device(): dec_sum = lax.psum(low(grad_dec_local), ('dp', 'mp')).astype(jnp.float32)]
    psum x1, waiting for transfers between devices: 82.7 us -> 53.4 us  [per_device(): qkv_sum = lax.psum(low(grad_qkv_local), 'dp').astype(jnp.float32)]
    all_to_all x1, waiting for transfers between devices: 0.01 us -> 14.2 us  [per_device(): lax.all_to_all(outgoing.reshape(data_par, capacity, dec_width), 'dp', spl...]
    reduce_sum x0 -> x1, other arithmetic: none -> 11.5 us  [per_device(): jnp.sum(lax.all_gather(low(grad_dec_local), ('dp', 'mp')), axis=0)]
  transfers between devices with their start and end apart: 15 -> 15, of which waited for: 10 -> 11; matrix products, arithmetic and copies ran while one was open for 19% -> 20% of each run, Pallas kernels for 0% -> 0%
where the time goes in v1:
time: 790 us; the launch traced here: 780 us
  waiting for transfers between devices  386 us (49%)
  blocking collectives  136 us (17%)
  matrix products  119 us (15%)
  other arithmetic  64.2 us (8%)
  local copies, waits for them, and re-layouts  34.5 us (4%)
  starting transfers between devices  16.8 us (2%)
  between operations  14.8 us (2%)
  loops' own time  8.46 us (1%)
    all_gather x1, waiting for transfers between devices, per_device(): lax.all_gather(low(grad_dec_local), ('dp', 'mp'))  147 us
    psum x1, waiting for transfers between devices, per_device(): qkv_sum = lax.psum(low(grad_qkv_local), 'dp').astype(jnp.float32)  53.4 us
    all_gather x1, waiting for transfers between devices, per_device(): norm2_all = lax.all_gather(normed2, 'mp', axis=0, tiled=True)  42.9 us
    psum x1, blocking collectives, per_device(): lax.psum((jnp.sum(grad_hat, axis=0), jnp.sum(grad_hat * band_hat, axis=0)...  42.8 us
    reduce_scatter x1, waiting for transfers between devices, per_device(): lax.psum_scatter(low(jnp.einsum('tf,df->td', grad_pre, up_weight, preferr...  42.3 us
    psum x1, blocking collectives, per_device(): lax.psum((jnp.sum(inputs_f, axis=0), jnp.sum(inputs_f * inputs_f, axis=0)...  42.1 us
    reduce_scatter x1, waiting for transfers between devices, per_device(): lax.psum_scatter(low(jnp.einsum('tcj,dcj->td', grad_triples, qkv_weight,...  33.4 us
    all_gather x1, blocking collectives, gather_rows(): column = lax.all_gather(mine, 'mp', axis=0)  16.9 us
  transfers between devices with their start and end apart: 15, of which 11 were waited for; matrix products, arithmetic and copies ran while one was open for 20% of the time, Pallas kernels for 0%

profile of v1, /device:TPU:0, one launch (start us, length us, event | category | flops | bytes accessed | tf_op | source)
XLA Modules:
  0.0 780.1 jit_solution(11948669551419301176)
XLA Ops:
  8.6 42.1 %all-reduce.1 = (f32[1024]{0:T(1024)S(1)}, f32[1024]{0:T(1024)S(1)}) all-reduce(f32[1024]{0:T(1024)S(1)} %get-tuple-element.181, f32[1024]{0:T(1024)S(1)} %get-tuple-element.180), channel_id=1, replica_groups=mesh['dp'=8,'mp'=4] {'dp','mp'}, use_global_device_ids=true, to_apply=%region_6.7 | all-reduce | flops 2048 | bytes 16384 | tf_op jit(solution)/shard_map/psum | solution.py:72
  59.7 4.2 all-to-all-start.2
  64.8 16.9 %all-gather = bf16[128,1024]{1,0:T(8,128)(2,1)} all-gather(bf16[32,1024]{1,0:T(8,128)(2,1)S(1)} %constant_dynamic-slice_fusion), channel_id=2, replica_groups=mesh['dp'=8,'mp'=4] {'mp'}, dimensions={0}, use_global_device_ids=true | all-gather | bytes 327680 | tf_op jit(solution)/shard_map/all_gather | solution.py:25
  81.8 10.6 %all-gather.4 = s32[4,1,256]{2,1,0:T(1,128)S(1)} all-gather(s32[1,1,256]{2,1,0:T(1,128)S(1)} %bitcast.167), channel_id=1, replica_groups=mesh['dp'=8,'mp'=4] {'mp'}, dimensions={0}, use_global_device_ids=true | all-gather | bytes 5120 | tf_op jit(solution)/shard_map/all_gather | solution.py:82
  93.5 13.1 %all-gather.11.cloned.1.call-done = bf16[1024,1024]{1,0:T(8,128)(2,1)} async-done(((bf16[256,1024]{1,0:T(8,128)(2,1)}), bf16[1024,1024]{1,0:T(8,128)(2,1)}) %all-gather.11.cloned.1.call-update) | async-done | bytes 2097168 | tf_op jit(solution)/shard_map/all_gather | solution.py:81
  106.6 3.9 add_convert_fusion.1
  112.2 22.3 %while.27 = (s32[]{:T(128)}, bf16[2,512,4,64]{1,3,2,0:T(8,128)(2,1)}, f32[2,4,512]{2,1,0:T(4,128)S(1)}, s32[2]{0:T(128)S(1)}, s32[1024]{0:T(1024)S(1)}, /*index=...) while((s32[]{:T(128)}, ...), condition=%wide.region_12.13_spmd, body=%wide.region_9.12_spmd.sunk | while | flops 562690048 | bytes 35203332 | solution.py:114
  142.5 4.1 all-to-all-start
  149.7 3.2 copy.77
  152.9 8.4 %all-to-all-done = bf16[4,256,256]{1,2,0:T(8,128)(2,1)} async-done(((bf16[4,256,256]{1,2,0:T(8,128)(2,1)}), bf16[4,256,256]{1,2,0:T(8,128)(2,1)}, u32[]{:S(2)}, u32[]{:S(2)}) %all-to-all-start) | async-done | bytes 524320 | tf_op jit(solution)/shard_map/all_to_all | solution.py:116
  166.1 13.0 %all-gather.15.cloned.1.call-done = bf16[1024,512]{1,0:T(8,128)(2,1)} async-done(((bf16[256,512]{1,0:T(8,128)(2,1)}), bf16[1024,512]{1,0:T(8,128)(2,1)}) %all-gather.15.cloned.1.call-update) | async-done | bytes 1048592 | tf_op jit(solution)/shard_map/all_gather | solution.py:179
  179.1 4.1 convolution_convert_fusion.4
  183.2 42.9 %all-gather.13.cloned.1.call-done = bf16[1024,1024]{1,0:T(8,128)(2,1)} async-done(((bf16[256,1024]{1,0:T(8,128)(2,1)}), bf16[1024,1024]{1,0:T(8,128)(2,1)}) %all-gather.13.cloned.1.call-update) | async-done | bytes 2097168 | tf_op jit(solution)/shard_map/all_gather | solution.py:120
  226.1 4.7 fusion.106
  230.9 13.9 %convert_reduce_fusion = (f32[1024]{0:T(1024)}, bf16[1024,1024]{1,0:T(8,128)(2,1)S(1)}, f32[1024,1024]{1,0:T(8,128)}) fusion(f32[1024,1024]{1,0:T(8,128)S(1)} %fusion.106, f32[1024]{0:T(1024)S(1)} %convert_element_type.186, bf16[1024,1024]{1,0:T(8,128)(2,1)S(1)} %copy-done.66, bf16[1024,1024]{1,0:T(8,128)(2,1)S(1)} %copy-done), kind=kOutput, calls=%fused_computation.48 | convolution fusion | flops 2226125824 | bytes 14688256 | tf_op jit(solution)/shard_map/tc,fc->tf/dot_general | solution.py:191
  246.1 3.7 convolution_convert_fusion.3
  250.2 42.3 %reduce-scatter.8.cloned.1.call-done = bf16[256,1024]{1,0:T(8,128)(2,1)} async-done(((bf16[1024,1024]{1,0:T(8,128)(2,1)}), bf16[256,1024]{1,0:T(8,128)(2,1)}) %reduce-scatter.8.cloned.1.call-update) | async-done | bytes 524304 | tf_op jit(solution)/shard_map/reduce_scatter | solution.py:202
  300.0 3.1 convolution_convert_fusion.2
  303.1 4.6 multiply_convert_fusion.1
  307.7 3.7 convolution_convert_fusion.5
  311.4 3.7 convolution_convert_fusion
  316.7 3.5 all-to-all-start.3
  320.2 4.1 convolution_convert_fusion.6
  324.4 6.0 convolution_convert_fusion.1
  330.5 4.1 all-to-all-done.3
  338.6 45.7 %while.28 = (s32[]{:T(128)}, f32[1024,4,64]{0,2,1:T(8,128)S(1)}, f32[1024,4,64]{0,2,1:T(8,128)}, bf16[2,512,4,64]{1,3,2,0:T(8,128)(2,1)}, s32[2]{0:T(128)S(1)}, ...) while((s32[]{:T(128)}, f32[1024,4,64]{0,2,1:T(8,128)S(1)}, ...), condition=%wide.region_21.22_spmd.clone, body=%wide.region_19.21_spmd.clone.sunk | while | flops 1375729664 | bytes 164432320 | solution.py:258
  343.5 3.3 multiply_reduce_fusion.3
  346.8 3.7 multiply_convert_fusion.3
  350.5 3.5 fusion.181
  355.4 3.6 fusion.182
  365.6 3.3 multiply_reduce_fusion.3
  369.0 3.7 multiply_convert_fusion.3
  372.7 3.4 fusion.181
  377.4 4.8 fusion.182
  387.6 4.6 fusion.50
  393.2 4.6 bitcast_convert_fusion
  397.8 3.3 fusion.107
  405.5 4.1 all-to-all-start.1
  411.2 14.2 %all-to-all-done.1 = bf16[8,64,512]{2,1,0:T(8,128)(2,1)S(1)} async-done(((bf16[8,64,512]{2,1,0:T(8,128)(2,1)}), bf16[8,64,512]{2,1,0:T(8,128)(2,1)S(1)}, u32[]{:S(2)}, u32[]{:S(2)}) %all-to-all-start.1) | async-done | bytes 524320 | tf_op jit(solution)/shard_map/all_to_all | solution.py:149
  428.7 13.3 %all-reduce.2 = (f32[2,256]{1,0:T(2,128)}, f32[1024]{0:T(1024)}) all-reduce(f32[2,256]{1,0:T(2,128)S(1)} %pad_maximum_fusion.2, f32[1024]{0:T(1024)S(1)} %copy-done.56), channel_id=1, replica_groups=mesh['dp'=8,'mp'=4] {'dp'}, use_global_device_ids=true, to_apply=%region_35.36 | all-reduce | flops 1536 | bytes 12288 | tf_op jit(solution)/shard_map/psum | solution.py:287
  442.0 53.4 %all-reduce.6.cloned.1.call-done = (bf16[1024,3,256]{2,0,1:T(8,128)(2,1)}, bf16[1024,1024]{1,0:T(8,128)(2,1)}, bf16[1024,1024]{1,0:T(8,128)(2,1)}) async-done(((bf16[1024,3,256]{2,0,1:T(8,128)(2,1)}, bf16[1024,1024]{1,0:T(8,128)(2,1)}, bf16[1024,1024]{1,0:T(8,128)(2,1)}), (bf16[1024,3,256]{2,0,1:T(8,128)(2,1)}, bf16[1024,1024]{1,0:T(8,128)(2,1)}, bf16[1024,1024]{1,0:T(8,128)(2,1)})) %all-reduce.6.cloned.1.call-update) | async-done | bytes 5767184 | tf_op jit(solution)/shard_map/psum | solution.py:282
  495.4 3.5 convert_element_type.210
  504.0 13.8 %reduce-scatter.14.cloned.1.call-done = bf16[1,32,1024]{2,1,0:T(8,128)(2,1)} async-done(((bf16[4,32,1024]{2,1,0:T(8,128)(2,1)}), bf16[1,32,1024]{2,1,0:T(8,128)(2,1)}) %reduce-scatter.14.cloned.1.call-update) | async-done | bytes 65552 | tf_op jit(solution)/shard_map/reduce_scatter | solution.py:218
  517.8 10.1 %all-gather.2 = bf16[1,256,1024]{2,1,0:T(8,128)(2,1)S(1)} all-gather(bf16[1,32,1024]{2,1,0:T(8,128)(2,1)} %reduce-scatter.14.cloned.1.call-done), channel_id=4, replica_groups=mesh['dp'=8,'mp'=4] {'dp'}, dimensions={1}, use_global_device_ids=true | all-gather | bytes 589824 | tf_op jit(solution)/shard_map/all_gather | solution.py:219
  529.0 33.4 %reduce-scatter.10.cloned.1.call-done = bf16[256,1024]{1,0:T(8,128)(2,1)} async-done(((bf16[1024,1024]{1,0:T(8,128)(2,1)}), bf16[256,1024]{1,0:T(8,128)(2,1)}) %reduce-scatter.10.cloned.1.call-update) | async-done | bytes 524304 | tf_op jit(solution)/shard_map/reduce_scatter | solution.py:274
  568.4 42.8 %all-reduce = (f32[1024]{0:T(1024)S(1)}, f32[1024]{0:T(1024)S(1)}, f32[1024]{0:T(1024)}, f32[1024]{0:T(1024)}, f32[1024]{0:T(1024)}, /*index=5*/f32[1024]{0:T(10...) all-reduce(f32[1024]{0:T(1024)S(1)} %get-tuple-element.176, ...), channel_id=1, replica_groups=mesh['dp'=8,'mp'=4] {'dp','mp'}, use_global_device_ids=true, to_apply=%region_28.29 | all-reduce | flops 9216 | bytes 73728 | tf_op jit(solution)/shard_map/psum | solution.py:288
  613.6 146.6 %all-gather.19.cloned.1.call-done = bf16[32768,512]{1,0:T(8,128)(2,1)} async-done(((bf16[1024,512]{1,0:T(8,128)(2,1)}), bf16[32768,512]{1,0:T(8,128)(2,1)}) %all-gather.19.cloned.1.call-update) | async-done | bytes 33554448 | tf_op jit(solution)/shard_map/all_gather | solution.py:286
  760.3 11.5 %reduce_sum.306 = bf16[1024,512]{1,0:T(8,128)(2,1)S(1)} reduce(bf16[32,1024,512]{2,1,0:T(8,128)(2,1)} %bitcast.153, bf16[]{:T(256)} %constant.79.clone.1), dimensions={0}, to_apply=%region_50.51 | reduce | flops 16252928 | bytes 34603008 | tf_op jit(solution)/shard_map/reduce_sum | solution.py:286
  (280 shorter events, 104.5 us)
Async XLA Ops:
  7.2 223.6 %copy-start = (bf16[1024,1024]{1,0:T(8,128)(2,1)S(1)}, bf16[1024,1024]{1,0:T(8,128)(2,1)}, u32[]{:S(2)}) copy-start(bf16[1024,1024]{1,0:T(8,128)(2,1)} %param.39) | copy-start | bytes 6291460
  7.2 74.6 %copy-start.60 = (s32[256]{0:T(256)S(1)}, s32[256]{0:T(256)}, u32[]{:S(2)}) copy-start(s32[256]{0:T(256)} %param.26) | copy-start | bytes 3076
  7.2 85.2 %copy-start.59 = (f32[2,256]{1,0:T(2,128)S(1)}, f32[2,256]{1,0:T(2,128)}, u32[]{:S(2)}) copy-start(f32[2,256]{1,0:T(2,128)} %param.32) | copy-start | bytes 6148
  7.2 85.2 %copy-start.50 = (s32[256]{0:T(256)S(1)}, s32[256]{0:T(256)}, u32[]{:S(2)}) copy-start(s32[256]{0:T(256)} %param.27) | copy-start | bytes 3076
  7.2 99.4 %all-gather.11.cloned.1.call-start = ((), (), s32[]{:S(2)}) async-start(), calls=%async_computation.9 | async-start | bytes 2621440 | tf_op jit(solution)/shard_map/all_gather | solution.py:81
  50.7 110.6 %copy-start.34 = (f32[1024]{0:T(1024)}, f32[1024]{0:T(1024)S(1)}, u32[]{:S(2)}) copy-start(f32[1024]{0:T(1024)S(1)} %get-tuple-element.257) | copy-start | bytes 12292
  50.7 110.6 %copy-start.36 = (f32[1024]{0:T(1024)}, f32[1024]{0:T(1024)S(1)}, u32[]{:S(2)}) copy-start(f32[1024]{0:T(1024)S(1)} %get-tuple-element.258) | copy-start | bytes 12292
  59.7 82.8 %all-to-all-start.2 = ((bf16[8,64,512]{2,1,0:T(8,128)(2,1)}), bf16[8,64,512]{2,1,0:T(8,128)(2,1)}, u32[]{:S(2)}, u32[]{:S(2)}) async-start(bf16[8,64,512]{2,1,0:T(8,128)(2,1)} %bitcast.21), calls=%async_computation.3 | async-start | bytes 1048576 | tf_op jit(solution)/shard_map/all_to_all | solution.py:156
  63.9 85.8 %all-gather.17.cloned.1.call-start = ((), (), s32[]{:S(2)}) async-start(), calls=%async_computation.17 | async-start | bytes 2359296 | tf_op jit(solution)/shard_map/all_gather | solution.py:26
  134.6 18.4 %copy-start.5 = (bf16[1024,4,64]{0,2,1:T(8,128)(2,1)}, bf16[1024,4,64]{0,2,1:T(8,128)(2,1)S(1)}, u32[]{:S(2)}) copy-start(bf16[1024,4,64]{0,2,1:T(8,128)(2,1)S(1)} %get-tuple-element.482) | copy-start | bytes 1572868
  137.7 23.6 %copy-start.7 = (bf16[256,1024]{1,0:T(8,128)(2,1)S(1)}, bf16[256,1024]{1,0:T(8,128)(2,1)}, u32[]{:S(2)}) copy-start(bf16[256,1024]{1,0:T(8,128)(2,1)} %param.25) | copy-start | bytes 1572868
  137.7 23.6 %copy-start.42 = (f32[1024]{0:T(1024)S(1)}, f32[1024]{0:T(1024)}, u32[]{:S(2)}) copy-start(f32[1024]{0:T(1024)} %param.34) | copy-start | bytes 12292
  142.5 18.8 %all-to-all-start = ((bf16[4,256,256]{1,2,0:T(8,128)(2,1)}), bf16[4,256,256]{1,2,0:T(8,128)(2,1)}, u32[]{:S(2)}, u32[]{:S(2)}) async-start(bf16[4,256,256]{1,2,0:T(8,128)(2,1)} %copy.76), calls=%async_computation | async-start | bytes 1048576 | tf_op jit(solution)/shard_map/all_to_all | solution.py:116
  146.7 32.4 %all-gather.15.cloned.1.call-start = ((), (), s32[]{:S(2)}) async-start(), calls=%async_computation.12 | async-start | bytes 1310720 | tf_op jit(solution)/shard_map/all_gather | solution.py:179
  146.9 17.0 %copy-start.61 = (s32[256]{0:T(256)}, s32[256]{0:T(256)S(1)}, u32[]{:S(2)}) copy-start(s32[256]{0:T(256)S(1)} %multiply_add_fusion.2) | copy-start | bytes 3076
  149.6 76.5 %all-gather.13.cloned.1.call-start = ((), (), s32[]{:S(2)}) async-start(), calls=%async_computation.10 | async-start | bytes 2621440 | tf_op jit(solution)/shard_map/all_gather | solution.py:120
  149.7 15.2 %copy-start.39 = (f32[1024]{0:T(1024)S(1)}, f32[1024]{0:T(1024)}, u32[]{:S(2)}) copy-start(f32[1024]{0:T(1024)} %param.35) | copy-start | bytes 12292
  149.7 15.2 %copy-start.53 = (f32[1024]{0:T(1024)S(1)}, f32[1024]{0:T(1024)}, u32[]{:S(2)}) copy-start(f32[1024]{0:T(1024)} %param.36) | copy-start | bytes 12292
  166.0 126.5 %reduce-scatter.8.cloned.1.call-start = ((), (), s32[]{:S(2)}) async-start(), calls=%async_computation.13 | async-start | bytes 2621440 | tf_op jit(solution)/shard_map/reduce_scatter | solution.py:202
  230.9 15.3 %copy-start.63 = (bf16[1024,1024]{1,0:T(8,128)(2,1)S(1)}, bf16[1024,1024]{1,0:T(8,128)(2,1)}, u32[]{:S(2)}) copy-start(bf16[1024,1024]{1,0:T(8,128)(2,1)} %param.37) | copy-start | bytes 6291460
  246.1 46.3 %copy-start.12 = (f32[256,1024]{1,0:T(8,128)S(1)}, f32[256,1024]{1,0:T(8,128)}, u32[]{:S(2)}) copy-start(f32[256,1024]{1,0:T(8,128)} %copy-done.11) | copy-start | bytes 3145732
  249.9 47.2 %copy-start.23 = (bf16[256,512]{1,0:T(8,128)(2,1)S(1)}, bf16[256,512]{1,0:T(8,128)(2,1)}, u32[]{:S(2)}) copy-start(bf16[256,512]{1,0:T(8,128)(2,1)} %get-tuple-element.254) | copy-start | bytes 786436
  249.9 142.4 %reduce-scatter.12.cloned.1.call-start = ((), (), s32[]{:S(2)}) async-start(), calls=%async_computation.15 | async-start | bytes 2359296 | tf_op jit(solution)/shard_map/reduce_scatter | solution.py:217
  316.7 17.8 %all-to-all-start.3 = ((bf16[256,4,256]{2,0,1:T(8,128)(2,1)}), bf16[256,4,256]{2,0,1:T(8,128)(2,1)S(1)}, u32[]{:S(2)}, u32[]{:S(2)}) async-start(bf16[256,4,256]{2,0,1:T(8,128)(2,1)} %bitcast.120), calls=%async_computation.5 | async-start | bytes 1048576 | tf_op jit(solution)/shard_map/all_to_all | solution.py:220
  320.2 82.5 %reduce-scatter.6.cloned.1.call-start = ((), (), s32[]{:S(2)}) async-start(), calls=%async_computation.11 | async-start | bytes 1310720 | tf_op jit(solution)/shard_map/reduce_scatter | solution.py:127
  324.3 14.3 %copy-start.6 = (bf16[1024,4,64]{0,2,1:T(8,128)(2,1)S(1)}, bf16[1024,4,64]{0,2,1:T(8,128)(2,1)}, u32[]{:S(2)}) copy-start(bf16[1024,4,64]{0,2,1:T(8,128)(2,1)} %copy-done.5) | copy-start | bytes 1572868
  324.3 14.3 %copy-start.10 = (bf16[1024,4,64]{0,2,1:T(8,128)(2,1)S(1)}, bf16[1024,4,64]{0,2,1:T(8,128)(2,1)}, u32[]{:S(2)}) copy-start(bf16[1024,4,64]{0,2,1:T(8,128)(2,1)} %copy-done.9) | copy-start | bytes 1572868
  324.4 171.0 %all-reduce.6.cloned.1.call-start = ((), (), s32[]{:S(2)}) async-start(), calls=%async_computation.19 | async-start | bytes 11534336 | tf_op jit(solution)/shard_map/psum | solution.py:282
  392.3 125.6 %reduce-scatter.14.cloned.1.call-start = ((), (), s32[]{:S(2)}) async-start(), calls=%async_computation.16 | async-start | bytes 327680 | tf_op jit(solution)/shard_map/reduce_scatter | solution.py:218
  393.0 169.4 %reduce-scatter.10.cloned.1.call-start = ((), (), s32[]{:S(2)}) async-start(), calls=%async_computation.14 | async-start | bytes 2621440 | tf_op jit(solution)/shard_map/reduce_scatter | solution.py:274
  397.8 362.5 %all-gather.19.cloned.1.call-start = ((), (), s32[]{:S(2)}) async-start(), calls=%async_computation.18 | async-start | bytes 34603008 | tf_op jit(solution)/shard_map/all_gather | solution.py:286
  402.6 22.7 %copy-start.65 = (f32[512]{0:T(512)S(1)}, f32[512]{0:T(512)}, u32[]{:S(2)}) copy-start(f32[512]{0:T(512)} %param.43) | copy-start | bytes 6148
  405.5 23.2 %copy-start.56 = (f32[1024]{0:T(1024)S(1)}, f32[1024]{0:T(1024)}, u32[]{:S(2)}) copy-start(f32[1024]{0:T(1024)} %get-tuple-element.237) | copy-start | bytes 12292
  405.5 19.8 %all-to-all-start.1 = ((bf16[8,64,512]{2,1,0:T(8,128)(2,1)}), bf16[8,64,512]{2,1,0:T(8,128)(2,1)S(1)}, u32[]{:S(2)}, u32[]{:S(2)}) async-start(bf16[8,64,512]{2,1,0:T(8,128)(2,1)} %bitcast.19), calls=%async_computation.2 | async-start | bytes 1048576 | tf_op jit(solution)/shard_map/all_to_all | solution.py:149
  501.4 61.0 %copy-start.8 = (bf16[256,1024]{1,0:T(8,128)(2,1)S(1)}, bf16[256,1024]{1,0:T(8,128)(2,1)}, u32[]{:S(2)}) copy-start(bf16[256,1024]{1,0:T(8,128)(2,1)} %param.25) | copy-start | bytes 1572868
  501.4 61.0 %copy-start.35 = (f32[1024]{0:T(1024)S(1)}, f32[1024]{0:T(1024)}, u32[]{:S(2)}) copy-start(f32[1024]{0:T(1024)} %copy-done.34) | copy-start | bytes 12292
  501.4 61.0 %copy-start.37 = (f32[1024]{0:T(1024)S(1)}, f32[1024]{0:T(1024)}, u32[]{:S(2)}) copy-start(f32[1024]{0:T(1024)} %copy-done.36) | copy-start | bytes 12292
  501.4 61.0 %copy-start.38 = (f32[1024]{0:T(1024)S(1)}, f32[1024]{0:T(1024)}, u32[]{:S(2)}) copy-start(f32[1024]{0:T(1024)} %param.29) | copy-start | bytes 12292
  501.4 61.0 %copy-start.41 = (f32[256]{0:T(256)S(1)}, f32[256]{0:T(256)}, u32[]{:S(2)}) copy-start(f32[256]{0:T(256)} %copy-done.40) | copy-start | bytes 3076
  501.4 62.5 %copy-start.49 = (f32[256]{0:T(256)S(1)}, f32[256]{0:T(256)}, u32[]{:S(2)}) copy-start(f32[256]{0:T(256)} %copy-done.48) | copy-start | bytes 3076
  501.4 62.5 %copy-start.47 = (f32[256]{0:T(256)S(1)}, f32[256]{0:T(256)}, u32[]{:S(2)}) copy-start(f32[256]{0:T(256)} %copy-done.46) | copy-start | bytes 3076
  501.4 64.2 %copy-start.17 = (f32[256,1024]{1,0:T(8,128)S(1)}, f32[256,1024]{1,0:T(8,128)}, u32[]{:S(2)}) copy-start(f32[256,1024]{1,0:T(8,128)} %copy-done.16) | copy-start | bytes 3145732
  501.5 64.2 %copy-start.22 = (f32[256,1024]{1,0:T(8,128)S(1)}, f32[256,1024]{1,0:T(8,128)}, u32[]{:S(2)}) copy-start(f32[256,1024]{1,0:T(8,128)} %get-tuple-element.264) | copy-start | bytes 3145732
  501.5 64.2 %copy-start.52 = (f32[256]{0:T(256)S(1)}, f32[256]{0:T(256)}, u32[]{:S(2)}) copy-start(f32[256]{0:T(256)} %copy-done.51) | copy-start | bytes 3076
  504.0 64.4 %copy-start.43 = (f32[1024]{0:T(1024)S(1)}, f32[1024]{0:T(1024)}, u32[]{:S(2)}) copy-start(f32[1024]{0:T(1024)} %get-tuple-element.171) | copy-start | bytes 12292
  504.0 64.4 %copy-start.44 = (f32[1024]{0:T(1024)S(1)}, f32[1024]{0:T(1024)}, u32[]{:S(2)}) copy-start(f32[1024]{0:T(1024)} %get-tuple-element.177) | copy-start | bytes 12292
  504.0 64.4 %copy-start.45 = (f32[1024]{0:T(1024)S(1)}, f32[1024]{0:T(1024)}, u32[]{:S(2)}) copy-start(f32[1024]{0:T(1024)} %get-tuple-element.240) | copy-start | bytes 12292
  504.0 64.4 %copy-start.58 = (f32[512]{0:T(512)S(1)}, f32[512]{0:T(512)}, u32[]{:S(2)}) copy-start(f32[512]{0:T(512)} %get-tuple-element.253) | copy-start | bytes 6148
  (46 other events, 175.9 us)
Sparse Core Ops, SparseCore 0:
  56.8 49.7 all-gather.10
  108.5 26.6 all-gather.16
  149.7 29.2 all-gather.14
  181.1 45.0 all-gather.12
  250.0 42.4 reduce-scatter.7
  303.2 40.3 reduce-scatter.11
  346.4 27.3 reduce-scatter.5
  392.4 102.9 all-reduce.5
  497.7 20.0 reduce-scatter.13
  520.5 41.8 reduce-scatter.9
  565.3 194.8 all-gather.18
